TPU v7x, 512 devices: a whole 4x8x8 slice. The times are simulated.
512 devices in a mesh: dp: 8 (over y), expert: 64 (over x, z, core).
Axes of the slice: x: 4, y: 8, z: 8, core: 2. Of those that a mesh axis runs over, the one named last changes fastest.
Arguments:
- tokens: bfloat16 [8192, 3584], P('expert', 'dp'), may hold values from -6 to 6
- cotangent: bfloat16 [8192, 3584], P('expert', 'dp'), may hold values from -12 to 12
- expert_ids: int32 [8192, 8], P('expert'), may hold values from 0 to 63, all different within a row; in each aligned block of 128 rows (0 to 127, 128 to 255, ...) at most 16 rows name the same one
- gate_levels: int32 [8192, 8], P('expert'), may hold values from 1 to 15
- capacity: int32 [64], replicated, may hold values from 4 to 16, as said below
- up_weight: bfloat16 [64, 3584, 1024], P('expert', 'dp'), may hold values from -0.09375 to 0.09375
- down_weight: bfloat16 [64, 3584, 1024], P('expert', 'dp'), may hold values from -0.1875 to 0.1875
Outputs:
- token_grad: bfloat16 [8192, 3584], P('expert', 'dp')
- up_grad: bfloat16 [64, 3584, 1024], P('expert', 'dp')
- down_grad: bfloat16 [64, 3584, 1024], P('expert', 'dp')
Inputs may be any that keep to these rules, and one draw needn't show every extreme that they name: `expert_ids`: in each aligned block of 128 tokens every expert is named by exactly 16 choices. `capacity`: some expert accepts 16 rows and some only 4.
All inputs are finite; a program needn't handle non-finite values.
Results may differ from a plain program's by a relative error of at most 0.023.
Values may be sent and summed in bfloat16 or wider, within the bound.
A program may use at most 64 MiB of HBM per device.

v0:
```python
import jax
import jax.numpy as jnp
from jax import lax
from jax.sharding import PartitionSpec as P


def silu_slope(preact):
    sigmoid = jax.nn.sigmoid(preact)
    return sigmoid * (1.0 + preact * (1.0 - sigmoid))


def per_device(tokens, cotangent, expert_ids, gate_levels, capacity, up_weight, down_weight):
    tok_rows, width_dev = tokens.shape
    top_count = expert_ids.shape[1]
    expert_count = capacity.shape[0]
    slots = tok_rows * top_count // expert_count
    row_count = expert_count * slots
    flat_ids = expert_ids.reshape(-1)
    expert_column = jnp.arange(expert_count, dtype=jnp.int32)[:, None]
    onehot = (flat_ids[None, :] == expert_column).astype(jnp.int32)
    earlier = jnp.cumsum(onehot, axis=1) - onehot
    slot_rank = jnp.sum(earlier * onehot, axis=0)
    limits = jnp.sum(onehot * capacity[:, None], axis=0)
    slot_index = jnp.where(slot_rank < limits, flat_ids * slots + slot_rank, -1).reshape(
        tok_rows, top_count
    )
    levels = gate_levels.astype(jnp.float32)
    gate_weights = levels / jnp.sum(levels, axis=1, keepdims=True)
    targets = jnp.arange(row_count, dtype=jnp.int32)[:, None]
    placing = jnp.zeros((row_count, tok_rows), jnp.float32)
    weighted = jnp.zeros((row_count, tok_rows), jnp.float32)
    for choice_index in range(top_count):
        matched = slot_index[:, choice_index][None, :] == targets
        placing = placing + matched.astype(jnp.float32)
        weighted = weighted + jnp.where(matched, gate_weights[:, choice_index][None, :], 0.0)
    slot_gate = jnp.sum(weighted, axis=1)
    placing_half = placing.astype(jnp.bfloat16)
    send_rows = jnp.dot(placing_half, tokens, preferred_element_type=jnp.float32).astype(
        jnp.bfloat16
    )
    placed_cot = jnp.dot(placing_half, cotangent, preferred_element_type=jnp.float32)
    send_cot = (slot_gate[:, None] * placed_cot).astype(jnp.bfloat16)
    block_shape = (expert_count, slots, width_dev)
    arrived_rows, arrived_cot = (
        lax.all_to_all(
            send_rows.reshape(block_shape), "expert", split_axis=0, concat_axis=0, tiled=True
        ),
        lax.all_to_all(
            send_cot.reshape(block_shape), "expert", split_axis=0, concat_axis=0, tiled=True
        ),
    )
    expert_in = arrived_rows.reshape(row_count, width_dev)
    expert_cot = arrived_cot.reshape(row_count, width_dev)
    weight_up = up_weight[0]
    weight_down = down_weight[0]
    pre_part = jnp.dot(expert_in, weight_up, preferred_element_type=jnp.float32)
    cot_part = jnp.dot(expert_cot, weight_down, preferred_element_type=jnp.float32)
    contract_rows = (((0,), (0,)), ((), ()))
    contract_hidden = (((1,), (1,)), ((), ()))
    preact, hidden_cot = (
        lax.psum_scatter(
            pre_part.astype(jnp.bfloat16), "dp", scatter_dimension=1, tiled=True
        ).astype(jnp.float32),
        lax.psum_scatter(
            cot_part.astype(jnp.bfloat16), "dp", scatter_dimension=1, tiled=True
        ).astype(jnp.float32),
    )
    hidden = jax.nn.silu(preact).astype(jnp.bfloat16)
    act_cot = (hidden_cot * silu_slope(preact)).astype(jnp.bfloat16)
    hidden_piece = lax.all_gather(hidden, "dp", axis=1, tiled=True)
    cot_piece = lax.all_gather(act_cot, "dp", axis=1, tiled=True)
    up_term = lax.dot_general(
        expert_in, cot_piece, contract_rows, preferred_element_type=jnp.float32
    )
    down_term = lax.dot_general(
        expert_cot, hidden_piece, contract_rows, preferred_element_type=jnp.float32
    )
    back_term = lax.dot_general(
        cot_piece, weight_up, contract_hidden, preferred_element_type=jnp.float32
    )
    back_rows = back_term.astype(jnp.bfloat16).reshape(block_shape)
    returned = lax.all_to_all(back_rows, "expert", split_axis=0, concat_axis=0, tiled=True)
    token_grad = lax.dot_general(
        placing_half,
        returned.reshape(row_count, width_dev),
        contract_rows,
        preferred_element_type=jnp.float32,
    ).astype(jnp.bfloat16)
    up_grad = up_term.astype(jnp.bfloat16)[None]
    down_grad = down_term.astype(jnp.bfloat16)[None]
    return (token_grad, up_grad, down_grad)


def solution(mesh):
    return jax.shard_map(
        per_device,
        mesh=mesh,
        in_specs=(
            P("expert", "dp"),
            P("expert", "dp"),
            P("expert", None),
            P("expert", None),
            P(),
            P("expert", "dp", None),
            P("expert", "dp", None),
        ),
        out_specs=(P("expert", "dp"), P("expert", "dp", None), P("expert", "dp", None)),
        check_vma=False,
    )
```

profile of v0, /device:TPU:1, one launch (start us, length us, event | category | flops | bytes accessed | tf_op | source)
XLA Modules:
  0.0 279.2 jit_solution(4377099423747551868)
XLA Ops:
  7.2 0.0 copy-start
  7.2 0.0 copy-start.3
  7.2 0.0 copy-start.6
  7.2 0.0 reduce-scatter.9.cloned.1.call-start
  7.2 0.9 copy.46
  8.1 0.1 eq.145
  8.2 0.1 eq.149
  8.3 0.8 select_reduce_fusion
  9.1 0.1 reduce_sum.43
  9.2 18.0 %reduce-window.6 = s32[64,8,128]{2,1,0:T(8,128)S(1)} reduce-window(s32[64,8,128]{2,1,0:T(8,128)S(1)} %fusion.13, s32[]{:T(128)} %constant.5.clone.1), window={size=1x1x128 pad=0_0x0_0x127_0}, to_apply=%region_0.0 | reduce-window | flops 8323072 | bytes 524292 | tf_op jit(solution)/shard_map/reduce-window
  27.2 0.1 slice.72
  27.4 0.1 copy.47
  27.6 0.1 copy.48
  27.7 0.1 select_reduce_fusion.1
  27.8 0.1 reduce_sum.41
  27.9 0.0 copy-done.3
  28.0 0.0 copy-done.6
  28.0 0.7 convolution_convert_fusion.2
  28.7 0.5 copy.54
  29.3 43.2 %all_to_all.15 = bf16[64,16,448]{2,1,0:T(8,128)(2,1)S(1)} all-to-all(bf16[64,16,448]{2,1,0:T(8,128)(2,1)S(1)} %bitcast.67), channel_id=1, replica_groups=mesh['dp'=8,'expert'=64] {'expert'}, dimensions={0} | all-to-all | bytes 1835008 | tf_op jit(solution)/shard_map/all_to_all | solution.py:45
  72.4 0.0 copy-done
  72.4 2.6 convolution_convert_fusion
  75.0 3.9 %copy.58 = bf16[1024,1024]{0,1:T(8,128)(2,1)} copy(bf16[1024,1024]{1,0:T(8,128)(2,1)} %convolution_convert_fusion) | data formatting | bytes 4194304
  78.9 0.0 copy-start.4
  78.9 0.0 copy-start.7
  78.9 0.0 reduce-scatter.9.cloned.1.call-update
  79.0 0.0 reduce-scatter.7.cloned.1.call-start
  79.0 0.6 copy-done.4
  79.7 0.5 add_reduce_fusion
  80.2 0.0 copy-done.7
  80.2 1.7 multiply_convert_fusion
  81.8 1.5 copy.53
  83.3 0.0 copy-start.5
  83.3 34.7 %all_to_all.16 = bf16[64,16,448]{2,1,0:T(8,128)(2,1)S(1)} all-to-all(bf16[64,16,448]{2,1,0:T(8,128)(2,1)S(1)} %bitcast.68), channel_id=1, replica_groups=mesh['dp'=8,'expert'=64] {'expert'}, dimensions={0} | all-to-all | bytes 1835008 | tf_op jit(solution)/shard_map/all_to_all | solution.py:48
  118.0 0.0 copy-start.1
  118.0 1.0 copy-done.1
  119.0 0.0 copy-done.5
  119.0 2.6 convolution_convert_fusion.1
  121.6 3.9 %copy.56 = bf16[1024,1024]{0,1:T(8,128)(2,1)} copy(bf16[1024,1024]{1,0:T(8,128)(2,1)} %convolution_convert_fusion.1) | data formatting | bytes 4194304
  125.5 0.0 reduce-scatter.7.cloned.1.call-update
  125.5 0.0 all-gather.3.cloned.1.call-start
  125.6 0.0 reduce-scatter.9.cloned.1.call-done
  125.6 1.1 copy.59
  126.7 36.4 %reduce-scatter.7.cloned.1.call-done = bf16[128,1024]{1,0:T(8,128)(2,1)} async-done(((bf16[1024,1024]{1,0:T(8,128)(2,1)}), bf16[128,1024]{1,0:T(8,128)(2,1)}) %reduce-scatter.7.cloned.1.call-update) | async-done | bytes 262160
  163.1 1.1 copy.57
  164.2 1.0 fusion.12
  165.3 0.0 all-gather.3.cloned.1.call-update
  165.3 0.0 all-gather.5.cloned.1.call-start
  165.3 0.5 all-gather.5.cloned.1.call-update
  165.9 49.2 %all-gather.3.cloned.1.call-done = bf16[1024,1024]{1,0:T(8,128)(2,1)} async-done(((bf16[1024,128]{1,0:T(8,128)(2,1)}), bf16[1024,1024]{1,0:T(8,128)(2,1)}) %all-gather.3.cloned.1.call-update) | async-done | bytes 2097168 | tf_op jit(solution)/shard_map/all_gather | solution.py:71
  215.0 2.7 convolution_convert_fusion.5
  217.8 1.3 copy.55
  219.1 15.0 %all-to-all-start.2 = ((bf16[64,16,448]{2,1,0:T(8,128)(2,1)}), bf16[64,16,448]{2,1,0:T(8,128)(2,1)}, u32[]{:S(2)}, u32[]{:S(2)}) async-start(bf16[64,16,448]{2,1,0:T(8,128)(2,1)} %bitcast.23), calls=%async_computation.2 | async-start | bytes 2097152 | tf_op jit(solution)/shard_map/all_to_all | solution.py:82
  234.1 0.0 copy-start.2
  234.1 3.8 %fusion = bf16[1,448,1024]{2,1,0:T(8,128)(2,1)} fusion(bf16[1024,448]{1,0:T(8,128)(2,1)S(1)} %bitcast.70, bf16[1024,1024]{1,0:T(8,128)(2,1)} %all-gather.3.cloned.1.call-done), kind=kOutput, calls=%fused_computation.7 | convolution fusion | flops 939982848 | bytes 3932160 | tf_op jit(solution)/shard_map/dot_general | solution.py:72
  237.9 28.5 %all-gather.5.cloned.1.call-done = bf16[1024,1024]{1,0:T(8,128)(2,1)} async-done(((bf16[1024,128]{1,0:T(8,128)(2,1)}), bf16[1024,1024]{1,0:T(8,128)(2,1)}) %all-gather.5.cloned.1.call-update) | async-done | bytes 2097168 | tf_op jit(solution)/shard_map/all_gather | solution.py:70
  266.3 0.0 copy-done.2
  266.4 3.6 %fusion.1 = bf16[1,448,1024]{2,1,0:T(8,128)(2,1)} fusion(bf16[1024,448]{1,0:T(8,128)(2,1)S(1)} %bitcast.72, bf16[1024,1024]{1,0:T(8,128)(2,1)} %all-gather.5.cloned.1.call-done), kind=kOutput, calls=%fused_computation.8 | convolution fusion | flops 939982848 | bytes 3932160 | tf_op jit(solution)/shard_map/dot_general | solution.py:75
  270.0 0.0 all-to-all-done.2
  270.0 2.7 convolution_convert_fusion.6
  (10 shorter events, 0.2 us)
Async XLA Ops:
  7.2 65.3 %copy-start = (bf16[1,448,1024]{2,1,0:T(8,128)(2,1)S(1)}, bf16[1,448,1024]{2,1,0:T(8,128)(2,1)}, u32[]{:S(2)}) copy-start(bf16[1,448,1024]{2,1,0:T(8,128)(2,1)} %param.12) | copy-start | bytes 2752516
  7.2 20.8 %copy-start.3 = (s32[128,8]{0,1:T(8,128)S(1)}, s32[128,8]{0,1:T(8,128)}, u32[]{:S(2)}) copy-start(s32[128,8]{0,1:T(8,128)} %param.9) | copy-start | bytes 12292
  7.2 20.8 %copy-start.6 = (bf16[128,448]{0,1:T(8,128)(2,1)S(1)}, bf16[128,448]{0,1:T(8,128)(2,1)}, u32[]{:S(2)}) copy-start(bf16[128,448]{0,1:T(8,128)(2,1)} %param.7) | copy-start | bytes 344068
  7.2 118.4 %reduce-scatter.9.cloned.1.call-start = ((), (), s32[]{:S(2)}) async-start(), calls=%async_computation.8 | async-start | bytes 2359296
  78.9 0.7 copy-start.4
  78.9 1.2 copy-start.7
  79.0 84.1 %reduce-scatter.7.cloned.1.call-start = ((), (), s32[]{:S(2)}) async-start(), calls=%async_computation.7 | async-start | bytes 2359296
  83.3 35.7 %copy-start.5 = (bf16[1,448,1024]{2,1,0:T(8,128)(2,1)S(1)}, bf16[1,448,1024]{2,1,0:T(8,128)(2,1)}, u32[]{:S(2)}) copy-start(bf16[1,448,1024]{2,1,0:T(8,128)(2,1)} %param.13) | copy-start | bytes 2752516
  118.0 1.0 copy-start.1
  125.5 89.5 %all-gather.3.cloned.1.call-start = ((), (), s32[]{:S(2)}) async-start(), calls=%async_computation.5 | async-start | bytes 2359296 | tf_op jit(solution)/shard_map/all_gather | solution.py:71
  165.3 101.0 %all-gather.5.cloned.1.call-start = ((), (), s32[]{:S(2)}) async-start(), calls=%async_computation.6 | async-start | bytes 2359296 | tf_op jit(solution)/shard_map/all_gather | solution.py:70
  219.1 50.9 %all-to-all-start.2 = ((bf16[64,16,448]{2,1,0:T(8,128)(2,1)}), bf16[64,16,448]{2,1,0:T(8,128)(2,1)}, u32[]{:S(2)}, u32[]{:S(2)}) async-start(bf16[64,16,448]{2,1,0:T(8,128)(2,1)} %bitcast.23), calls=%async_computation.2 | async-start | bytes 2097152 | tf_op jit(solution)/shard_map/all_to_all | solution.py:82
  234.1 32.3 %copy-start.2 = (bf16[64,16,448]{2,1,0:T(8,128)(2,1)S(1)}, bf16[64,16,448]{2,1,0:T(8,128)(2,1)}, u32[]{:S(2)}) copy-start(bf16[64,16,448]{2,1,0:T(8,128)(2,1)} %copy-done.1) | copy-start | bytes 2752516
Sparse Core Ops, SparseCore 0:
  79.1 37.3 reduce-scatter.8
  125.6 37.4 reduce-scatter.6
  165.7 49.2 all-gather.2
  217.5 48.8 all-gather.4
where the time goes:
time: 284 us; the launch traced here: 279 us
  waiting for transfers between devices  115 us (40%)
  blocking collectives  77.9 us (27%)
  other arithmetic  20.6 us (7%)
  matrix products  20.4 us (7%)
  local copies, waits for them, and re-layouts  16.7 us (6%)
  starting transfers between devices  15.1 us (5%)
  between operations  14 us (5%)
    all_gather x1, waiting for transfers between devices, per_device(): cot_piece = lax.all_gather(act_cot, 'dp', axis=1, tiled=True)  49.2 us
    all_to_all x1, blocking collectives, per_device(): lax.all_to_all(send_rows.reshape(block_shape), 'expert', split_axis=0, co...  43.2 us
    unnamed x6, waiting for transfers between devices  37 us
    all_to_all x1, blocking collectives, per_device(): lax.all_to_all(send_cot.reshape(block_shape), 'expert', split_axis=0, con...  34.7 us
    all_gather x1, waiting for transfers between devices, per_device(): hidden_piece = lax.all_gather(hidden, 'dp', axis=1, tiled=True)  28.5 us
    another operation x2, other arithmetic  18 us
    all_to_all x1, starting transfers between devices, per_device(): lax.all_to_all(back_rows, 'expert', split_axis=0, concat_axis=0, tiled=True)  15 us
    unnamed x21, local copies, waits for them, and re-layouts  12.6 us
  transfers between devices with their start and end apart: 5, of which 3 were waited for; matrix products, arithmetic and copies ran while one was open for 8% of the time, Pallas kernels for 0%

commit v1 on v0

v1 whole, which is shorter than its diff:
```python
import functools

import jax
import jax.numpy as jnp
from jax import lax
from jax.experimental import pallas as pl
from jax.experimental.pallas import tpu as pltpu
from jax.sharding import PartitionSpec as P

MESH = pl.DeviceIdType.MESH
NN = (((1,), (0,)), ((), ()))
NT = (((1,), (1,)), ((), ()))
TN = (((0,), (0,)), ((), ()))
SPACING = 4


def matmul(left, right, dims=NN):
    return lax.dot_general(left, right, dims, preferred_element_type=jnp.float32)


def layer_kernel(
    groups,
    members,
    ring,
    slots,
    tokens_ref,
    cot_ref,
    ids_ref,
    levels_ref,
    capacity_ref,
    up_hbm,
    down_hbm,
    token_grad_ref,
    up_grad_hbm,
    down_grad_hbm,
    send_ref,
    recv_ref,
    recv_turned,
    placing_ref,
    rank_ref,
    level_ref,
    up_ref,
    down_ref,
    part_ref,
    sums_ref,
    full_ref,
    back_ref,
    returned_ref,
    combined_ref,
    up_grad_ref,
    down_grad_ref,
    local_sem,
    out_send,
    out_recv,
    sum_send,
    sum_recv,
    full_send,
    full_recv,
    back_send,
    back_recv,
):
    experts = groups * members
    width, tok_rows = tokens_ref.shape
    hidden = up_ref.shape[1]
    piece = hidden // ring
    depth = up_ref.shape[0]
    chunk = members * slots
    top = ids_ref.shape[0]
    me_dp = lax.axis_index("dp")
    me = lax.axis_index("expert")
    my_group = lax.div(me, members)
    my_member = lax.rem(me, members)
    after = lax.rem(me_dp + 1, ring)
    before = lax.rem(me_dp + ring - 1, ring)
    longest = ring // 2

    def reach(matrix, direction):
        far = matrix == direction
        return longest if far else ring - 1 - longest

    def hop_slot(matrix, direction, hop):
        return (hop - 1) if direction == 0 else reach(matrix, 0) + hop - 1

    def neighbour(direction):
        return {"dp": after if direction == 0 else before}

    def ring_index(offset):
        return lax.rem(me_dp + offset + ring, ring)

    barrier = pltpu.get_barrier_semaphore()

    def greet(step, carry):
        pl.semaphore_signal(
            barrier,
            inc=1,
            device_id={"expert": lax.rem(me + step, experts)},
            device_id_type=MESH,
        )
        return carry

    lax.fori_loop(1, experts, greet, 0)
    for direction in range(2):
        pl.semaphore_signal(barrier, inc=1, device_id=neighbour(direction), device_id_type=MESH)

    up_rows = pl.ds(0, width)
    down_rows = pl.ds(depth - width, width)
    load_up = pltpu.make_async_copy(up_hbm, up_ref.at[up_rows], local_sem.at[0])
    load_down = pltpu.make_async_copy(down_hbm, down_ref.at[down_rows], local_sem.at[1])
    load_up.start()
    load_down.start()
    up_ref[pl.ds(width, depth - width), :] = jnp.zeros((depth - width, hidden), jnp.bfloat16)
    down_ref[pl.ds(0, depth - width), :] = jnp.zeros((depth - width, hidden), jnp.bfloat16)

    ids = ids_ref[...]
    levels = levels_ref[...]
    expert_row = lax.broadcasted_iota(jnp.int32, (experts, tok_rows), 0)
    named = jnp.zeros((experts, tok_rows), jnp.float32)
    level = jnp.zeros((experts, tok_rows), jnp.float32)
    for choice in range(top):
        hit = ids[choice : choice + 1, :] == expert_row
        named = named + jnp.where(hit, 1.0, 0.0)
        level = level + jnp.where(hit, levels[choice : choice + 1, :].astype(jnp.float32), 0.0)
    total = jnp.sum(levels.astype(jnp.float32), axis=0, keepdims=True)
    earlier = lax.broadcasted_iota(jnp.int32, (tok_rows, tok_rows), 0) < lax.broadcasted_iota(
        jnp.int32, (tok_rows, tok_rows), 1
    )
    rank = matmul(named.astype(jnp.bfloat16), jnp.where(earlier, 1.0, 0.0).astype(jnp.bfloat16))
    diagonal = lax.broadcasted_iota(jnp.int32, (experts, experts), 0) == lax.broadcasted_iota(
        jnp.int32, (experts, experts), 1
    )
    limit = jnp.sum(
        jnp.where(diagonal, capacity_ref[...].astype(jnp.float32), 0.0), axis=1, keepdims=True
    )
    kept = (named > 0.0) & (rank < limit)
    rank_ref[...] = jnp.where(kept, rank, -1.0).astype(jnp.bfloat16)
    level_ref[...] = level.astype(jnp.bfloat16)

    def out_base(step):
        return pl.multiple_of(lax.rem(my_group + step, groups) * chunk, chunk)

    def place(step):
        base = out_base(step)
        row = base + lax.broadcasted_iota(jnp.int32, (chunk, experts), 0)
        column = lax.broadcasted_iota(jnp.int32, (chunk, experts), 1)
        mine = lax.div(row, slots) == column
        spread = jnp.where(mine, 1.0, 0.0).astype(jnp.bfloat16)
        slot = lax.rem(lax.broadcasted_iota(jnp.int32, (chunk, tok_rows), 0), slots)
        matched = matmul(spread, rank_ref[...]) == slot.astype(jnp.float32)
        placing = jnp.where(matched, 1.0, 0.0)
        slot_level = jnp.sum(placing * matmul(spread, level_ref[...]), axis=1, keepdims=True)
        slot_total = jnp.sum(placing * total, axis=1, keepdims=True)
        gate = jnp.where(slot_total > 0.0, slot_level / jnp.maximum(slot_total, 1.0), 0.0)
        placing = placing.astype(jnp.bfloat16)
        placing_ref[pl.ds(base, chunk), :] = placing
        both = jnp.concatenate([tokens_ref[...], cot_ref[...]], axis=0)
        rows = matmul(placing, both, NT)
        in_cot = lax.broadcasted_iota(jnp.int32, (chunk, 2 * width), 1) >= width
        rows = jnp.where(in_cot, gate * rows, rows)
        send_ref[pl.ds(base, chunk), :] = rows.astype(jnp.bfloat16)
        if step == 0:
            own = pl.multiple_of(me * slots, slots)
            to = pl.multiple_of(my_member * slots, slots)
            recv_ref[pl.ds(to, slots), :] = send_ref[pl.ds(own, slots), :]

    def send_out(step):
        group = lax.rem(my_group + step, groups)

        def one(index, carry):
            peer = group * members + lax.rem(my_member + index, members)
            pltpu.make_async_remote_copy(
                src_ref=send_ref.at[pl.ds(pl.multiple_of(peer * slots, slots), slots)],
                dst_ref=recv_ref.at[
                    pl.ds(pl.multiple_of(step * chunk + my_member * slots, slots), slots)
                ],
                send_sem=out_send,
                recv_sem=out_recv.at[step],
                device_id={"expert": peer},
                device_id_type=MESH,
            ).start()
            return carry

        lax.fori_loop(1 if step == 0 else 0, members, one, 0)

    def wait_for(ref, sem):
        pltpu.make_async_copy(ref, ref, sem).wait()

    def chunk_rows(step):
        return pl.ds(step * chunk, chunk)

    def arrived_rows(step):
        return pl.ds(0, chunk - slots if step == 0 else chunk)

    def ring_copy(source, target, send_sem, recv_sem, direction):
        pltpu.make_async_remote_copy(
            src_ref=source,
            dst_ref=target,
            send_sem=send_sem,
            recv_sem=recv_sem,
            device_id=neighbour(direction),
            device_id_type=MESH,
        ).start()

    routes = [(matrix, direction) for matrix in range(2) for direction in range(2)]

    def sum_hop(step, matrix, direction, hop):
        offset = reach(matrix, direction) - hop + 1
        owner = ring_index(offset if direction == 0 else -offset)
        slot = hop_slot(matrix, direction, hop)
        if hop > 1:
            came = hop_slot(matrix, direction, hop - 1)
            wait_for(sums_ref.at[step, matrix, came], sum_recv.at[step, matrix, came])
            part_ref[step, matrix, owner] = (
                part_ref[step, matrix, owner].astype(jnp.float32)
                + sums_ref[step, matrix, came].astype(jnp.float32)
            ).astype(jnp.bfloat16)
        ring_copy(
            part_ref.at[step, matrix, owner],
            sums_ref.at[step, matrix, slot],
            sum_send,
            sum_recv.at[step, matrix, slot],
            direction,
        )

    def summed(step, matrix):
        value = part_ref[step, matrix, me_dp].astype(jnp.float32)
        for direction in range(2):
            came = hop_slot(matrix, direction, reach(matrix, direction))
            wait_for(sums_ref.at[step, matrix, came], sum_recv.at[step, matrix, came])
            value = value + sums_ref[step, matrix, came].astype(jnp.float32)
        return value

    def full_wait(step, matrix, direction, hop):
        owner = ring_index(-hop if direction == 0 else hop)
        came = hop_slot(matrix, direction, hop)
        wait_for(full_ref.at[step, matrix, owner], full_recv.at[step, matrix, came])

    def full_hop(step, matrix, direction, hop):
        offset = hop - 1
        owner = ring_index(-offset if direction == 0 else offset)
        if hop > 1:
            full_wait(step, matrix, direction, hop - 1)
        slot = hop_slot(matrix, direction, hop)
        ring_copy(
            full_ref.at[step, matrix, owner],
            full_ref.at[step, matrix, owner],
            full_send,
            full_recv.at[step, matrix, slot],
            direction,
        )

    def forward(step):
        wait_for(recv_ref.at[arrived_rows(step)], out_recv.at[step])
        if step == 0:
            load_up.wait()
            load_down.wait()
        for matrix in range(2):
            weight = up_ref if matrix == 0 else down_ref
            start = 0 if matrix == 0 else 2 * width - depth

            def columns(block, carry, matrix=matrix, weight=weight, start=start):
                where = pl.ds(pl.multiple_of(block * 2 * piece, 2 * piece), 2 * piece)
                terms = matmul(recv_ref[chunk_rows(step), start : start + depth], weight[:, where])
                terms = terms.astype(jnp.bfloat16)
                part_ref[step, matrix, 2 * block] = terms[:, :piece]
                part_ref[step, matrix, 2 * block + 1] = terms[:, piece:]
                return carry

            lax.fori_loop(0, ring // 2, columns, 0)
        for matrix, direction in routes:
            sum_hop(step, matrix, direction, 1)

    def turn(step):
        recv_turned[:, chunk_rows(step)] = recv_ref[chunk_rows(step), :].T

    def activate(step):
        preact = summed(step, 0)
        sigmoid = jax.nn.sigmoid(preact)
        full_ref[step, 0, me_dp] = (preact * sigmoid).astype(jnp.bfloat16)
        for direction in range(2):
            full_hop(step, 0, direction, 1)
        slope = sigmoid * (1.0 + preact * (1.0 - sigmoid))
        full_ref[step, 1, me_dp] = (summed(step, 1) * slope).astype(jnp.bfloat16)
        for direction in range(2):
            full_hop(step, 1, direction, 1)

    def backward(step):
        for direction in range(2):
            full_wait(step, 1, direction, reach(1, direction))
        act_cot = jnp.concatenate([full_ref[step, 1, index] for index in range(ring)], axis=1)
        rows = matmul(act_cot, up_ref[...], NT)
        back_ref[chunk_rows(step), :] = rows[:, :width].astype(jnp.bfloat16)
        own = pl.multiple_of(me * slots, slots)
        if step == 0:
            at = pl.multiple_of(my_member * slots, slots)
            returned_ref[pl.ds(own, slots), :] = back_ref[pl.ds(at, slots), :]
        group = lax.rem(my_group + groups - step, groups)

        def one(index, carry):
            member = lax.rem(my_member + index, members)
            pltpu.make_async_remote_copy(
                src_ref=back_ref.at[
                    pl.ds(pl.multiple_of(step * chunk + member * slots, slots), slots)
                ],
                dst_ref=returned_ref.at[pl.ds(own, slots)],
                send_sem=back_send,
                recv_sem=back_recv.at[step],
                device_id={"expert": group * members + member},
                device_id_type=MESH,
            ).start()
            return carry

        lax.fori_loop(1 if step == 0 else 0, members, one, 0)
        for direction in range(2):
            full_wait(step, 0, direction, reach(0, direction))

    def combine(step):
        wait_for(returned_ref.at[arrived_rows(step)], back_recv.at[step])
        base = out_base(step)
        rows = pl.ds(base, chunk)
        terms = matmul(placing_ref[rows, :], returned_ref[rows, :], TN)
        combined_ref[...] = terms if step == 0 else combined_ref[...] + terms

    def weight_grads():
        def columns(block, carry):
            where = pl.ds(pl.multiple_of(block * 2 * piece, 2 * piece), 2 * piece)

            def pieces(matrix):
                return jnp.concatenate(
                    [
                        jnp.concatenate(
                            [full_ref[step, matrix, 2 * block + half] for half in range(2)], axis=1
                        )
                        for step in range(groups)
                    ],
                    axis=0,
                )

            up_grad_ref[:, where] = matmul(recv_turned[:width, :], pieces(1)).astype(jnp.bfloat16)
            down_grad_ref[:, where] = matmul(recv_turned[width:, :], pieces(0)).astype(jnp.bfloat16)
            return carry

        lax.fori_loop(0, ring // 2, columns, 0)

    place(0)
    pl.semaphore_wait(barrier, experts + 1)
    send_out(0)
    for step in range(1, groups):
        place(step)
        send_out(step)

    def stage(step, number):
        if number == 0:
            forward(step)
        elif number < longest:
            for matrix, direction in routes:
                if number + 1 <= reach(matrix, direction):
                    sum_hop(step, matrix, direction, number + 1)
            if number == 1:
                turn(step)
        elif number == longest:
            activate(step)
        elif number < 2 * longest:
            for matrix, direction in routes:
                if number - longest + 1 <= reach(matrix, direction):
                    full_hop(step, matrix, direction, number - longest + 1)
        elif number == 2 * longest:
            backward(step)

    for tick in range((groups - 1) * SPACING + 2 * longest + 1):
        for step in range(groups):
            if 0 <= tick - step * SPACING <= 2 * longest:
                stage(step, tick - step * SPACING)

    weight_grads()
    store_up = pltpu.make_async_copy(up_grad_ref, up_grad_hbm, local_sem.at[0])
    store_down = pltpu.make_async_copy(down_grad_ref, down_grad_hbm, local_sem.at[1])
    store_up.start()
    store_down.start()
    for step in range(groups):
        combine(step)
    token_grad_ref[...] = combined_ref[...].T.astype(jnp.bfloat16)

    moved = pl.ds(0, experts * slots - slots)
    wait_for(send_ref.at[moved], out_send)
    wait_for(back_ref.at[moved], back_send)
    wait_for(part_ref.at[:, :, pl.ds(0, ring - 1)], sum_send)
    wait_for(full_ref.at[:, :, pl.ds(0, ring - 1)], full_send)
    store_up.wait()
    store_down.wait()


def per_device(
    groups, members, ring, tokens, cotangent, expert_ids, gate_levels, capacity, up_weight, down_weight
):
    tok_rows, width = tokens.shape
    experts = groups * members
    slots = tok_rows * expert_ids.shape[1] // experts
    rows = experts * slots
    chunk = members * slots
    hidden = up_weight.shape[2]
    piece = hidden // ring
    depth = -(-width // 128) * 128
    half = jnp.bfloat16
    vmem = pl.BlockSpec(memory_space=pltpu.VMEM)
    anywhere = pl.BlockSpec(memory_space=pl.ANY)
    dma = pltpu.SemaphoreType.DMA
    token_grad, up_grad, down_grad = pl.pallas_call(
        functools.partial(layer_kernel, groups, members, ring, slots),
        out_shape=(
            jax.ShapeDtypeStruct((width, tok_rows), half),
            jax.ShapeDtypeStruct((width, hidden), half),
            jax.ShapeDtypeStruct((width, hidden), half),
        ),
        in_specs=[vmem] * 5 + [anywhere] * 2,
        out_specs=(vmem, anywhere, anywhere),
        scratch_shapes=[
            pltpu.VMEM((rows, 2 * width), half),
            pltpu.VMEM((rows, 2 * width), half),
            pltpu.VMEM((2 * width, rows), half),
            pltpu.VMEM((rows, tok_rows), half),
            pltpu.VMEM((experts, tok_rows), half),
            pltpu.VMEM((experts, tok_rows), half),
            pltpu.VMEM((depth, hidden), half),
            pltpu.VMEM((depth, hidden), half),
            pltpu.VMEM((groups, 2, ring, chunk, piece), half),
            pltpu.VMEM((groups, 2, ring - 1, chunk, piece), half),
            pltpu.VMEM((groups, 2, ring, chunk, piece), half),
            pltpu.VMEM((rows, width), half),
            pltpu.VMEM((rows, width), half),
            pltpu.VMEM((tok_rows, width), jnp.float32),
            pltpu.VMEM((width, hidden), half),
            pltpu.VMEM((width, hidden), half),
            dma((2,)),
            dma,
            dma((groups,)),
            dma,
            dma((groups, 2, ring - 1)),
            dma,
            dma((groups, 2, ring - 1)),
            dma,
            dma((groups,)),
        ],
        compiler_params=pltpu.CompilerParams(
            collective_id=0, has_side_effects=True, vmem_limit_bytes=56 * 1024 * 1024
        ),
    )(
        tokens.T,
        cotangent.T,
        expert_ids.T,
        gate_levels.T,
        capacity.reshape(1, experts),
        up_weight[0],
        down_weight[0],
    )
    return token_grad.T, up_grad[None], down_grad[None]


def solution(mesh):
    ring, experts = mesh.shape["dp"], mesh.shape["expert"]
    groups = 4
    return jax.shard_map(
        functools.partial(per_device, groups, experts // groups, ring),
        mesh=mesh,
        in_specs=(
            P("expert", "dp"),
            P("expert", "dp"),
            P("expert", None),
            P("expert", None),
            P(),
            P("expert", "dp", None),
            P("expert", "dp", None),
        ),
        out_specs=(P("expert", "dp"), P("expert", "dp", None), P("expert", "dp", None)),
        check_vma=False,
    )
```

time: 284 us -> 144 us (0.51); the launches traced: 279 us -> 144 us
  Pallas kernels: 0 us -> 138 us
  waiting for transfers between devices: 115 us -> 0 us
  blocking collectives: 77.9 us -> 0 us
  other arithmetic: 20.6 us -> 0 us
  matrix products: 20.4 us -> 0 us
  starting transfers between devices: 15.1 us -> 0 us
  between operations: 14 us -> 0.64 us
  local copies, waits for them, and re-layouts: 16.7 us -> 4.72 us
    pallas_call x0 -> x1, Pallas kernels: none -> 138 us  [per_device(): pl.pallas_call(functools.partial(layer_kernel, groups, members, ring, slo...]
    all_to_all x2 -> x0, blocking collectives: 77.9 us -> none  [the longest x1 43.2 us: per_device(): lax.all_to_all(send_rows.reshape(block_shape), 'expert', split_axis=0, co...]
    all_gather x2 -> x0, waiting for transfers between devices: 77.6 us -> none  [the longest x1 49.2 us: per_device(): cot_piece = lax.all_gather(act_cot, 'dp', axis=1, tiled=True)]
    unnamed x6 -> x0, waiting for transfers between devices: 37 us -> none
    dot_general x8 -> x0, matrix products: 20.4 us -> none  [the longest x1 3.78 us: per_device(): lax.dot_general(expert_in, cot_piece, contract_rows, preferred_element_ty...]
    another operation x2 -> x0, other arithmetic: 18 us -> none
    all_to_all x1 -> x0, starting transfers between devices: 15 us -> none  [per_device(): lax.all_to_all(back_rows, 'expert', split_axis=0, concat_axis=0, tiled=True)]
    unnamed x21 -> x5, local copies, waits for them, and re-layouts: 12.6 us -> 4.72 us
  transfers between devices with their start and end apart: 5 -> 0, of which waited for: 3 -> 0; matrix products, arithmetic and copies ran while one was open for 8% -> 0% of each run, Pallas kernels for 0% -> 0%
where the time goes in v1:
time: 144 us
  Pallas kernels  138 us (96%)
  local copies, waits for them, and re-layouts  4.72 us (3%)
    pallas_call x1, Pallas kernels, per_device(): pl.pallas_call(functools.partial(layer_kernel, groups, members, ring, slo...  138 us
    unnamed x5, local copies, waits for them, and re-layouts  4.72 us

profile of v1, /device:TPU:1, one launch (start us, length us, event | category | flops | bytes accessed | tf_op | source)
XLA Modules:
  0.0 143.8 jit_solution(4213433400294672927)
XLA Ops:
  0.6 138.5 %shard_map.94 = (bf16[448,128]{1,0:T(8,128)(2,1)}, bf16[448,1024]{1,0:T(8,128)(2,1)}, bf16[448,1024]{1,0:T(8,128)(2,1)}) custom-call(bf16[448,128]{1,0:T(8,128)(2,1)} %bitcast.15, bf16[448,128]{1,0:T(8,128)(2,1)} %bitcast.16, s32[8,128]{1,0:T(8,128)} %bitcast.17, s32[8,128]{1,0:T(8,128)} %bitcast.18, s32[1,64]{1,0:T(1,128)} %bitcast.19, ...), custom_call_target="tpu_custom_call" | custom-call | tf_op jit(solution)/shard_map/pallas_call | solution.py:407
  139.1 1.6 %copy.13 = bf16[128,448]{0,1:T(8,128)(2,1)} copy(bf16[128,448]{0,1:T(8,128)(2,1)} %bitcast.14) | data formatting | bytes 229376
  140.7 0.0 copy-start
  140.7 2.2 %copy.14 = bf16[1,448,1024]{2,1,0:T(8,128)(2,1)} copy(bf16[1,448,1024]{2,1,0:T(8,128)(2,1)} %bitcast.13) | data formatting | bytes 1835008
  142.9 0.0 copy-done
  142.9 0.9 copy.15
Async XLA Ops:
  140.7 2.2 %copy-start = (bf16[448,1024]{1,0:T(8,128)(2,1)S(1)}, bf16[448,1024]{1,0:T(8,128)(2,1)}, u32[]{:S(2)}) copy-start(bf16[448,1024]{1,0:T(8,128)(2,1)} %get-tuple-element.8) | copy-start | bytes 2752516

commit v2 on v1

--- a/solution.py
+++ b/solution.py
@@ -11,7 +11,10 @@
 NN = (((1,), (0,)), ((), ()))
 NT = (((1,), (1,)), ((), ()))
 TN = (((0,), (0,)), ((), ()))
-SPACING = 4
+CHUNKS = 8
+STARTS = {2: (0, 3), 4: (0, 4, 7, 9), 8: (0, 1, 2, 4, 6, 8, 10, 11)}
+X_CHIPS, CORES = 4, 2
+CHUNK_ORDER = {1: (0,), 2: (0, 1), 4: (0, 2, 3, 1), 8: (0, 1, 4, 6, 7, 5, 3, 2)}
 
 
 def matmul(left, right, dims=NN):
@@ -19,8 +22,8 @@
 
 
 def layer_kernel(
-    groups,
-    members,
+    chunks,
+    z_chips,
     ring,
     slots,
     tokens_ref,
@@ -47,6 +50,7 @@
     back_ref,
     returned_ref,
     combined_ref,
+    grad_sums_ref,
     up_grad_ref,
     down_grad_ref,
     local_sem,
@@ -59,20 +63,27 @@
     back_send,
     back_recv,
 ):
-    experts = groups * members
+    experts = X_CHIPS * z_chips * CORES
     width, tok_rows = tokens_ref.shape
     hidden = up_ref.shape[1]
     piece = hidden // ring
     depth = up_ref.shape[0]
-    chunk = members * slots
+    distances = z_chips // chunks
+    layer = X_CHIPS * CORES * slots
+    chunk = distances * layer
     top = ids_ref.shape[0]
     me_dp = lax.axis_index("dp")
     me = lax.axis_index("expert")
-    my_group = lax.div(me, members)
-    my_member = lax.rem(me, members)
+    my_core = lax.rem(me, CORES)
+    my_z = lax.rem(lax.div(me, CORES), z_chips)
+    my_x = lax.div(me, CORES * z_chips)
     after = lax.rem(me_dp + 1, ring)
     before = lax.rem(me_dp + ring - 1, ring)
     longest = ring // 2
+
+    def distance(step, index):
+        number = CHUNK_ORDER[chunks][step] * distances + index
+        return (number + 1) // 2 * (1 if number % 2 else -1)
 
     def reach(matrix, direction):
         far = matrix == direction
@@ -135,57 +146,70 @@
     rank_ref[...] = jnp.where(kept, rank, -1.0).astype(jnp.bfloat16)
     level_ref[...] = level.astype(jnp.bfloat16)
 
-    def out_base(step):
-        return pl.multiple_of(lax.rem(my_group + step, groups) * chunk, chunk)
+    def chunk_rows(step):
+        return pl.ds(step * chunk, chunk)
 
     def place(step):
-        base = out_base(step)
-        row = base + lax.broadcasted_iota(jnp.int32, (chunk, experts), 0)
-        column = lax.broadcasted_iota(jnp.int32, (chunk, experts), 1)
-        mine = lax.div(row, slots) == column
+        row = lax.broadcasted_iota(jnp.int32, (chunk, 1), 0)
+        core = (row >> (slots.bit_length() - 1)) & (CORES - 1)
+        x_away = (row >> ((CORES * slots).bit_length() - 1)) & (X_CHIPS - 1)
+        z_away = jnp.zeros((chunk, 1), jnp.int32)
+        for index in range(distances):
+            here = (row >> (layer.bit_length() - 1)) == index
+            z_away = jnp.where(here, distance(step, index), z_away)
+        z_away = jnp.where((x_away & 1) == 1, -z_away, z_away)
+        x_to = (my_x + x_away) & (X_CHIPS - 1)
+        z_to = (my_z + z_away) & (z_chips - 1)
+        expert = (x_to * z_chips + z_to) * CORES + core
+        mine = expert == lax.broadcasted_iota(jnp.int32, (chunk, experts), 1)
         spread = jnp.where(mine, 1.0, 0.0).astype(jnp.bfloat16)
-        slot = lax.rem(lax.broadcasted_iota(jnp.int32, (chunk, tok_rows), 0), slots)
+        slot = lax.broadcasted_iota(jnp.int32, (chunk, tok_rows), 0) & (slots - 1)
         matched = matmul(spread, rank_ref[...]) == slot.astype(jnp.float32)
         placing = jnp.where(matched, 1.0, 0.0)
         slot_level = jnp.sum(placing * matmul(spread, level_ref[...]), axis=1, keepdims=True)
         slot_total = jnp.sum(placing * total, axis=1, keepdims=True)
         gate = jnp.where(slot_total > 0.0, slot_level / jnp.maximum(slot_total, 1.0), 0.0)
         placing = placing.astype(jnp.bfloat16)
-        placing_ref[pl.ds(base, chunk), :] = placing
+        placing_ref[chunk_rows(step), :] = placing
         both = jnp.concatenate([tokens_ref[...], cot_ref[...]], axis=0)
         rows = matmul(placing, both, NT)
         in_cot = lax.broadcasted_iota(jnp.int32, (chunk, 2 * width), 1) >= width
         rows = jnp.where(in_cot, gate * rows, rows)
-        send_ref[pl.ds(base, chunk), :] = rows.astype(jnp.bfloat16)
+        send_ref[chunk_rows(step), :] = rows.astype(jnp.bfloat16)
         if step == 0:
-            own = pl.multiple_of(me * slots, slots)
-            to = pl.multiple_of(my_member * slots, slots)
-            recv_ref[pl.ds(to, slots), :] = send_ref[pl.ds(own, slots), :]
+            own = pl.ds(pl.multiple_of(my_core * slots, slots), slots)
+            recv_ref[own, :] = send_ref[own, :]
+
+    def exchange(step, side, source, target, send_sem, recv_sem):
+        for index in range(distances):
+            base = step * chunk + index * layer
+
+            def one(turn, carry, index=index, base=base):
+                x_away = lax.div(turn, CORES)
+                core = lax.rem(my_core + turn, CORES)
+                z_away = distance(step, index) * (1 - 2 * lax.rem(x_away, 2))
+                x_to = lax.rem(my_x + side * x_away + X_CHIPS, X_CHIPS)
+                z_to = lax.rem(my_z + side * z_away + z_chips, z_chips)
+                place_from = base + (x_away * CORES + core) * slots
+                place_to = base + (x_away * CORES + my_core) * slots
+                pltpu.make_async_remote_copy(
+                    src_ref=source.at[pl.ds(pl.multiple_of(place_from, slots), slots)],
+                    dst_ref=target.at[pl.ds(pl.multiple_of(place_to, slots), slots)],
+                    send_sem=send_sem,
+                    recv_sem=recv_sem.at[step],
+                    device_id={"expert": (x_to * z_chips + z_to) * CORES + core},
+                    device_id_type=MESH,
+                ).start()
+                return carry
+
+            own = step == 0 and index == 0
+            lax.fori_loop(1 if own else 0, X_CHIPS * CORES, one, 0)
 
     def send_out(step):
-        group = lax.rem(my_group + step, groups)
-
-        def one(index, carry):
-            peer = group * members + lax.rem(my_member + index, members)
-            pltpu.make_async_remote_copy(
-                src_ref=send_ref.at[pl.ds(pl.multiple_of(peer * slots, slots), slots)],
-                dst_ref=recv_ref.at[
-                    pl.ds(pl.multiple_of(step * chunk + my_member * slots, slots), slots)
-                ],
-                send_sem=out_send,
-                recv_sem=out_recv.at[step],
-                device_id={"expert": peer},
-                device_id_type=MESH,
-            ).start()
-            return carry
-
-        lax.fori_loop(1 if step == 0 else 0, members, one, 0)
+        exchange(step, 1, send_ref, recv_ref, out_send, out_recv)
 
     def wait_for(ref, sem):
         pltpu.make_async_copy(ref, ref, sem).wait()
-
-    def chunk_rows(step):
-        return pl.ds(step * chunk, chunk)
 
     def arrived_rows(step):
         return pl.ds(0, chunk - slots if step == 0 else chunk)
@@ -257,15 +281,10 @@
             weight = up_ref if matrix == 0 else down_ref
             start = 0 if matrix == 0 else 2 * width - depth
 
-            def columns(block, carry, matrix=matrix, weight=weight, start=start):
-                where = pl.ds(pl.multiple_of(block * 2 * piece, 2 * piece), 2 * piece)
-                terms = matmul(recv_ref[chunk_rows(step), start : start + depth], weight[:, where])
-                terms = terms.astype(jnp.bfloat16)
-                part_ref[step, matrix, 2 * block] = terms[:, :piece]
-                part_ref[step, matrix, 2 * block + 1] = terms[:, piece:]
-                return carry
-
-            lax.fori_loop(0, ring // 2, columns, 0)
+            terms = matmul(recv_ref[chunk_rows(step), start : start + depth], weight[...])
+            terms = terms.astype(jnp.bfloat16)
+            for index in range(ring):
+                part_ref[step, matrix, index] = terms[:, index * piece : (index + 1) * piece]
         for matrix, direction in routes:
             sum_hop(step, matrix, direction, 1)
 
@@ -289,54 +308,34 @@
         act_cot = jnp.concatenate([full_ref[step, 1, index] for index in range(ring)], axis=1)
         rows = matmul(act_cot, up_ref[...], NT)
         back_ref[chunk_rows(step), :] = rows[:, :width].astype(jnp.bfloat16)
-        own = pl.multiple_of(me * slots, slots)
         if step == 0:
-            at = pl.multiple_of(my_member * slots, slots)
-            returned_ref[pl.ds(own, slots), :] = back_ref[pl.ds(at, slots), :]
-        group = lax.rem(my_group + groups - step, groups)
-
-        def one(index, carry):
-            member = lax.rem(my_member + index, members)
-            pltpu.make_async_remote_copy(
-                src_ref=back_ref.at[
-                    pl.ds(pl.multiple_of(step * chunk + member * slots, slots), slots)
-                ],
-                dst_ref=returned_ref.at[pl.ds(own, slots)],
-                send_sem=back_send,
-                recv_sem=back_recv.at[step],
-                device_id={"expert": group * members + member},
-                device_id_type=MESH,
-            ).start()
-            return carry
-
-        lax.fori_loop(1 if step == 0 else 0, members, one, 0)
+            own = pl.ds(pl.multiple_of(my_core * slots, slots), slots)
+            returned_ref[own, :] = back_ref[own, :]
+        exchange(step, -1, back_ref, returned_ref, back_send, back_recv)
         for direction in range(2):
             full_wait(step, 0, direction, reach(0, direction))
 
     def combine(step):
         wait_for(returned_ref.at[arrived_rows(step)], back_recv.at[step])
-        base = out_base(step)
-        rows = pl.ds(base, chunk)
+        rows = chunk_rows(step)
         terms = matmul(placing_ref[rows, :], returned_ref[rows, :], TN)
         combined_ref[...] = terms if step == 0 else combined_ref[...] + terms
 
-    def weight_grads():
+    def weight_grads(step):
         def columns(block, carry):
             where = pl.ds(pl.multiple_of(block * 2 * piece, 2 * piece), 2 * piece)
-
-            def pieces(matrix):
-                return jnp.concatenate(
-                    [
-                        jnp.concatenate(
-                            [full_ref[step, matrix, 2 * block + half] for half in range(2)], axis=1
-                        )
-                        for step in range(groups)
-                    ],
-                    axis=0,
-                )
-
-            up_grad_ref[:, where] = matmul(recv_turned[:width, :], pieces(1)).astype(jnp.bfloat16)
-            down_grad_ref[:, where] = matmul(recv_turned[width:, :], pieces(0)).astype(jnp.bfloat16)
+            for matrix in range(2):
+                rows = recv_turned[matrix * width : (matrix + 1) * width, chunk_rows(step)]
+                pieces = [full_ref[step, 1 - matrix, 2 * block + half] for half in range(2)]
+                terms = matmul(rows, jnp.concatenate(pieces, axis=1))
+                if step > 0:
+                    terms = terms + grad_sums_ref[matrix, :, where]
+                if step < chunks - 1:
+                    grad_sums_ref[matrix, :, where] = terms
+                elif matrix == 0:
+                    up_grad_ref[:, where] = terms.astype(jnp.bfloat16)
+                else:
+                    down_grad_ref[:, where] = terms.astype(jnp.bfloat16)
             return carry
 
         lax.fori_loop(0, ring // 2, columns, 0)
@@ -344,7 +343,7 @@
     place(0)
     pl.semaphore_wait(barrier, experts + 1)
     send_out(0)
-    for step in range(1, groups):
+    for step in range(1, chunks):
         place(step)
         send_out(step)
 
@@ -365,18 +364,20 @@
                     full_hop(step, matrix, direction, number - longest + 1)
         elif number == 2 * longest:
             backward(step)
-
-    for tick in range((groups - 1) * SPACING + 2 * longest + 1):
-        for step in range(groups):
-            if 0 <= tick - step * SPACING <= 2 * longest:
-                stage(step, tick - step * SPACING)
-
-    weight_grads()
+        elif number == 2 * longest + 1:
+            weight_grads(step)
+
+    starts = STARTS[chunks]
+    for tick in range(starts[-1] + 2 * longest + 2):
+        for step in range(chunks):
+            if 0 <= tick - starts[step] <= 2 * longest + 1:
+                stage(step, tick - starts[step])
+
     store_up = pltpu.make_async_copy(up_grad_ref, up_grad_hbm, local_sem.at[0])
     store_down = pltpu.make_async_copy(down_grad_ref, down_grad_hbm, local_sem.at[1])
     store_up.start()
     store_down.start()
-    for step in range(groups):
+    for step in range(chunks):
         combine(step)
     token_grad_ref[...] = combined_ref[...].T.astype(jnp.bfloat16)
 
@@ -389,14 +390,19 @@
     store_down.wait()
 
 
+def hand_over(*refs):
+    for source, target in zip(refs[:3], refs[3:]):
+        target[...] = source[...]
+
+
 def per_device(
-    groups, members, ring, tokens, cotangent, expert_ids, gate_levels, capacity, up_weight, down_weight
+    chunks, z_chips, ring, tokens, cotangent, expert_ids, gate_levels, capacity, up_weight, down_weight
 ):
     tok_rows, width = tokens.shape
-    experts = groups * members
+    experts = X_CHIPS * z_chips * CORES
     slots = tok_rows * expert_ids.shape[1] // experts
     rows = experts * slots
-    chunk = members * slots
+    chunk = rows // chunks
     hidden = up_weight.shape[2]
     piece = hidden // ring
     depth = -(-width // 128) * 128
@@ -404,13 +410,14 @@
     vmem = pl.BlockSpec(memory_space=pltpu.VMEM)
     anywhere = pl.BlockSpec(memory_space=pl.ANY)
     dma = pltpu.SemaphoreType.DMA
-    token_grad, up_grad, down_grad = pl.pallas_call(
-        functools.partial(layer_kernel, groups, members, ring, slots),
-        out_shape=(
-            jax.ShapeDtypeStruct((width, tok_rows), half),
-            jax.ShapeDtypeStruct((width, hidden), half),
-            jax.ShapeDtypeStruct((width, hidden), half),
-        ),
+    shapes = (
+        jax.ShapeDtypeStruct((width, tok_rows), half),
+        jax.ShapeDtypeStruct((width, hidden), half),
+        jax.ShapeDtypeStruct((width, hidden), half),
+    )
+    results = pl.pallas_call(
+        functools.partial(layer_kernel, chunks, z_chips, ring, slots),
+        out_shape=shapes,
         in_specs=[vmem] * 5 + [anywhere] * 2,
         out_specs=(vmem, anywhere, anywhere),
         scratch_shapes=[
@@ -422,23 +429,24 @@
             pltpu.VMEM((experts, tok_rows), half),
             pltpu.VMEM((depth, hidden), half),
             pltpu.VMEM((depth, hidden), half),
-            pltpu.VMEM((groups, 2, ring, chunk, piece), half),
-            pltpu.VMEM((groups, 2, ring - 1, chunk, piece), half),
-            pltpu.VMEM((groups, 2, ring, chunk, piece), half),
+            pltpu.VMEM((chunks, 2, ring, chunk, piece), half),
+            pltpu.VMEM((chunks, 2, ring - 1, chunk, piece), half),
+            pltpu.VMEM((chunks, 2, ring, chunk, piece), half),
             pltpu.VMEM((rows, width), half),
             pltpu.VMEM((rows, width), half),
             pltpu.VMEM((tok_rows, width), jnp.float32),
+            pltpu.VMEM((2, width, hidden), jnp.float32),
             pltpu.VMEM((width, hidden), half),
             pltpu.VMEM((width, hidden), half),
             dma((2,)),
             dma,
-            dma((groups,)),
+            dma((chunks,)),
             dma,
-            dma((groups, 2, ring - 1)),
+            dma((chunks, 2, ring - 1)),
             dma,
-            dma((groups, 2, ring - 1)),
+            dma((chunks, 2, ring - 1)),
             dma,
-            dma((groups,)),
+            dma((chunks,)),
         ],
         compiler_params=pltpu.CompilerParams(
             collective_id=0, has_side_effects=True, vmem_limit_bytes=56 * 1024 * 1024
@@ -452,14 +460,18 @@
         up_weight[0],
         down_weight[0],
     )
+    rows_of = [pl.BlockSpec((width // 4, out.shape[1]), lambda i: (i, 0)) for out in shapes]
+    token_grad, up_grad, down_grad = pl.pallas_call(
+        hand_over, out_shape=shapes, grid=(4,), in_specs=rows_of, out_specs=rows_of
+    )(*results)
     return token_grad.T, up_grad[None], down_grad[None]
 
 
 def solution(mesh):
     ring, experts = mesh.shape["dp"], mesh.shape["expert"]
-    groups = 4
+    z_chips = experts // (X_CHIPS * CORES)
     return jax.shard_map(
-        functools.partial(per_device, groups, experts // groups, ring),
+        functools.partial(per_device, min(CHUNKS, z_chips), z_chips, ring),
         mesh=mesh,
         in_specs=(
             P("expert", "dp"),

time: 144 us -> 127 us (0.88)
  Pallas kernels: 138 us -> 126 us
  local copies, waits for them, and re-layouts: 4.72 us -> 0 us
    pallas_call x1 -> x2, Pallas kernels: 138 us -> 126 us  [the longest x1 123 us: per_device(): pl.pallas_call(functools.partial(layer_kernel, chunks, z_chips, ring, slo...]
    unnamed x5 -> x0, local copies, waits for them, and re-layouts: 4.72 us -> none
where the time goes in v2:
time: 127 us
  Pallas kernels  126 us (99%)
    pallas_call x1, Pallas kernels, per_device(): pl.pallas_call(functools.partial(layer_kernel, chunks, z_chips, ring, slo...  123 us
    pallas_call x1, Pallas kernels, per_device(): pl.pallas_call(hand_over, out_shape=shapes, grid=(4,), in_specs=rows_of,...  3.8 us

profile of v2, /device:TPU:1, one launch (start us, length us, event | category | flops | bytes accessed | tf_op | source)
XLA Modules:
  0.0 127.0 jit_solution(8836991051691166222)
XLA Ops:
  0.6 122.6 %shard_map.94 = (bf16[448,128]{1,0:T(8,128)(2,1)}, bf16[448,1024]{1,0:T(8,128)(2,1)}, bf16[448,1024]{1,0:T(8,128)(2,1)}) custom-call(bf16[448,128]{1,0:T(8,128)(2,1)} %bitcast.12, bf16[448,128]{1,0:T(8,128)(2,1)} %bitcast.13, s32[8,128]{1,0:T(8,128)} %bitcast.14, s32[8,128]{1,0:T(8,128)} %bitcast.15, s32[1,64]{1,0:T(1,128)} %bitcast.16, ...), custom_call_target="tpu_custom_call" | custom-call | tf_op jit(solution)/shard_map/pallas_call | solution.py:418
  123.2 3.8 %shard_map.95 = (bf16[448,128]{1,0:T(8,128)(2,1)}, bf16[448,1024]{1,0:T(8,128)(2,1)}, bf16[448,1024]{1,0:T(8,128)(2,1)}) custom-call(bf16[448,128]{1,0:T(8,128)(2,1)} %get-tuple-element.9.refs_0_, bf16[448,1024]{1,0:T(8,128)(2,1)} %get-tuple-element.10.refs_1_, bf16[448,1024]{1,0:T(8,128)(2,1)} %get-tuple-element.11.refs_2_), custom_call_target="tpu_custom_call" | custom-call | tf_op jit(solution)/shard_map/pallas_call | solution.py:464

commit v3 on v2

--- a/solution.py
+++ b/solution.py
@@ -12,7 +12,7 @@
 NT = (((1,), (1,)), ((), ()))
 TN = (((0,), (0,)), ((), ()))
 CHUNKS = 8
-STARTS = {2: (0, 3), 4: (0, 4, 7, 9), 8: (0, 1, 2, 4, 6, 8, 10, 11)}
+STARTS = {2: (0, 3), 4: (0, 4, 7, 9), 8: (0, 1, 2, 3, 5, 7, 8, 9)}
 X_CHIPS, CORES = 4, 2
 CHUNK_ORDER = {1: (0,), 2: (0, 1), 4: (0, 2, 3, 1), 8: (0, 1, 4, 6, 7, 5, 3, 2)}
 
@@ -390,9 +390,25 @@
     store_down.wait()
 
 
-def hand_over(*refs):
-    for source, target in zip(refs[:3], refs[3:]):
-        target[...] = source[...]
+def hand_over(token_in, up_in, down_in, token_out, up_out, down_out, token, up, down, came, left):
+    blocks = came.shape[1]
+    rows = up.shape[0] // blocks
+    steps = []
+    for block in range(blocks):
+        at = pl.ds(block * rows, rows)
+        for index, (source, held, target) in enumerate(
+            [(up_in, up, up_out), (down_in, down, down_out), (token_in, token, token_out)]
+        ):
+            load = pltpu.make_async_copy(source.at[at], held.at[at], came.at[index, block])
+            store = pltpu.make_async_copy(held.at[at], target.at[at], left.at[index, block])
+            steps.append((load, store))
+    for load, store in steps:
+        load.start()
+    for load, store in steps:
+        load.wait()
+        store.start()
+    for load, store in steps:
+        store.wait()
 
 
 def per_device(
@@ -460,9 +476,12 @@
         up_weight[0],
         down_weight[0],
     )
-    rows_of = [pl.BlockSpec((width // 4, out.shape[1]), lambda i: (i, 0)) for out in shapes]
     token_grad, up_grad, down_grad = pl.pallas_call(
-        hand_over, out_shape=shapes, grid=(4,), in_specs=rows_of, out_specs=rows_of
+        hand_over,
+        out_shape=shapes,
+        in_specs=[anywhere] * 3,
+        out_specs=(anywhere,) * 3,
+        scratch_shapes=[pltpu.VMEM(out.shape, half) for out in shapes] + [dma((3, 2)), dma((3, 2))],
     )(*results)
     return token_grad.T, up_grad[None], down_grad[None]
 

time: 127 us -> 125 us (0.984)
  Pallas kernels: 126 us -> 124 us
    pallas_call x1, Pallas kernels: 3.8 us -> 2.37 us  [per_device(): pl.pallas_call(hand_over, out_shape=shapes, in_specs=[anywhere] * 3, out_...]
where the time goes in v3:
time: 125 us
  Pallas kernels  124 us (99%)
    pallas_call x1, Pallas kernels, per_device(): pl.pallas_call(functools.partial(layer_kernel, chunks, z_chips, ring, slo...  122 us

profile of v3, /device:TPU:1, one launch (start us, length us, event | category | flops | bytes accessed | tf_op | source)
XLA Modules:
  0.0 125.0 jit_solution(18090376542196670470)
XLA Ops:
  0.6 122.0 %shard_map.94 = (bf16[448,128]{1,0:T(8,128)(2,1)}, bf16[448,1024]{1,0:T(8,128)(2,1)}, bf16[448,1024]{1,0:T(8,128)(2,1)}) custom-call(bf16[448,128]{1,0:T(8,128)(2,1)} %bitcast.12, bf16[448,128]{1,0:T(8,128)(2,1)} %bitcast.13, s32[8,128]{1,0:T(8,128)} %bitcast.14, s32[8,128]{1,0:T(8,128)} %bitcast.15, s32[1,64]{1,0:T(1,128)} %bitcast.16, ...), custom_call_target="tpu_custom_call" | custom-call | tf_op jit(solution)/shard_map/pallas_call | solution.py:434
  122.6 2.4 %shard_map.95 = (bf16[448,128]{1,0:T(8,128)(2,1)}, bf16[448,1024]{1,0:T(8,128)(2,1)}, bf16[448,1024]{1,0:T(8,128)(2,1)}) custom-call(bf16[448,128]{1,0:T(8,128)(2,1)} %get-tuple-element.9.token_in, bf16[448,1024]{1,0:T(8,128)(2,1)} %get-tuple-element.10.up_in, bf16[448,1024]{1,0:T(8,128)(2,1)} %get-tuple-element.11.down_in), custom_call_target="tpu_custom_call" | custom-call | tf_op jit(solution)/shard_map/pallas_call | solution.py:479

commit v4 on v3

--- a/solution.py
+++ b/solution.py
@@ -224,7 +224,7 @@
             device_id_type=MESH,
         ).start()
 
-    routes = [(matrix, direction) for matrix in range(2) for direction in range(2)]
+    routes = [(0, 0), (1, 1), (1, 0), (0, 1)]
 
     def sum_hop(step, matrix, direction, hop):
         offset = reach(matrix, direction) - hop + 1

time: 125 us -> 125 us (level)
  no operation moved by 1% of the time
where the time goes in v4:
time: 125 us
  Pallas kernels  124 us (99%)
    pallas_call x1, Pallas kernels, per_device(): pl.pallas_call(functools.partial(layer_kernel, chunks, z_chips, ring, slo...  122 us

profile of v4, /device:TPU:1, one launch (start us, length us, event | category | flops | bytes accessed | tf_op | source)
XLA Modules:
  0.0 124.7 jit_solution(2827805494333333534)
XLA Ops:
  0.6 121.7 %shard_map.94 = (bf16[448,128]{1,0:T(8,128)(2,1)}, bf16[448,1024]{1,0:T(8,128)(2,1)}, bf16[448,1024]{1,0:T(8,128)(2,1)}) custom-call(bf16[448,128]{1,0:T(8,128)(2,1)} %bitcast.12, bf16[448,128]{1,0:T(8,128)(2,1)} %bitcast.13, s32[8,128]{1,0:T(8,128)} %bitcast.14, s32[8,128]{1,0:T(8,128)} %bitcast.15, s32[1,64]{1,0:T(1,128)} %bitcast.16, ...), custom_call_target="tpu_custom_call" | custom-call | tf_op jit(solution)/shard_map/pallas_call | solution.py:434
  122.4 2.4 %shard_map.95 = (bf16[448,128]{1,0:T(8,128)(2,1)}, bf16[448,1024]{1,0:T(8,128)(2,1)}, bf16[448,1024]{1,0:T(8,128)(2,1)}) custom-call(bf16[448,128]{1,0:T(8,128)(2,1)} %get-tuple-element.9.token_in, bf16[448,1024]{1,0:T(8,128)(2,1)} %get-tuple-element.10.up_in, bf16[448,1024]{1,0:T(8,128)(2,1)} %get-tuple-element.11.down_in), custom_call_target="tpu_custom_call" | custom-call | tf_op jit(solution)/shard_map/pallas_call | solution.py:479
